TPU v7x, 32 devices: a whole 2x2x4 slice. The times are simulated.
32 devices in a mesh: dp: 2 (over x), row: 4 (over y, core), col: 4 (over z).
Axes of the slice: x: 2, y: 2, z: 4, core: 2. Of those that a mesh axis runs over, the one named last changes fastest.
Arguments:
- inputs: bfloat16 [14568, 12, 128], P(('dp', 'row'), 'col'), may hold values from -15 to 15
- mixer_weight: float32 [768, 2304], P('row', 'col'), may hold values from -0.3125 to 0.3125
- mixer_bias: float32 [12, 128], P('col', 'row'), may hold values from -3 to 3
- merge_weight: float32 [768, 768], P(('col', 'row')), may hold values from -0.875 to 0.875
- merge_bias: float32 [12, 64], P('col', 'row'), may hold values from -3 to 3
- expand_weight: float32 [768, 3072], P('row', 'col'), may hold values from -0.21875 to 0.21875
- expand_bias: float32 [12, 256], P('col', 'row'), may hold values from -3 to 3
- reduce_weight: float32 [3072, 768], P(('col', 'row')), may hold values from -0.109375 to 0.109375
- reduce_bias: float32 [12, 64], P('col', 'row'), may hold values from -3 to 3
- first_gain: float32 [12, 64], P('col', 'row'), may hold values from 0.1 to 1.9
- first_shift: float32 [12, 64], P('col', 'row'), may hold values from -3 to 3
- second_gain: float32 [12, 64], P('col', 'row'), may hold values from 0.1 to 1.9
- second_shift: float32 [12, 64], P('col', 'row'), may hold values from -3 to 3
- cotangent: bfloat16 [14568, 12, 128], P(('dp', 'row'), 'col'), may hold values from -6 to 6
Outputs:
- outputs: bfloat16 [14568, 12, 128], P(('dp', 'row'), 'col')
- input_grad: float32 [14568, 12, 128], P(('dp', 'row'), 'col')
- grad_mixer_weight: float32 [768, 2304], P('row', 'col')
- grad_mixer_bias: float32 [12, 128], P('col', 'row')
- grad_merge_weight: float32 [768, 768], P(('col', 'row'))
- grad_merge_bias: float32 [12, 64], P('col', 'row')
- grad_expand_weight: float32 [768, 3072], P('row', 'col')
- grad_expand_bias: float32 [12, 256], P('col', 'row')
- grad_reduce_weight: float32 [3072, 768], P(('col', 'row'))
- grad_reduce_bias: float32 [12, 64], P('col', 'row')
- grad_first_gain: float32 [12, 64], P('col', 'row')
- grad_first_shift: float32 [12, 64], P('col', 'row')
- grad_second_gain: float32 [12, 64], P('col', 'row')
- grad_second_shift: float32 [12, 64], P('col', 'row')
All inputs are finite; a program needn't handle non-finite values.
Results may differ from a plain program's by a relative error of at most 0.012.
The roundings to bfloat16 on the way count: a program that leaves them out, or rounds other values in their place, can miss the bound.
Values may be sent and summed in bfloat16 or wider, within the bound.
A program may use at most 192 MiB of HBM per device.

v0:
```python
import jax
import jax.numpy as jnp
from jax import lax
from jax.sharding import PartitionSpec as P

D = 768
HD = 64
LEN = 1214
EPSILON = 1e-06


def to_rows(values):
    halves = values.shape[0]
    groups = values.shape[1]
    return (
        values.reshape(halves, groups, 2, HD).transpose(0, 2, 1, 3).reshape(2 * halves, groups * HD)
    )


def from_rows(values):
    halves = values.shape[0] // 2
    groups = values.shape[1] // HD
    return (
        values.reshape(halves, 2, groups, HD).transpose(0, 2, 1, 3).reshape(halves, groups, 2 * HD)
    )


def exact_gelu(values):
    return jax.nn.gelu(values, approximate=False)


def inner_rows(left, right):
    return lax.dot_general(
        left, right, (((0,), (0,)), ((), ())), preferred_element_type=jnp.float32
    )


def times_transposed(left, right):
    return lax.dot_general(
        left, right, (((1,), (1,)), ((), ())), preferred_element_type=jnp.float32
    )


def as_vector(values):
    return values.astype(jnp.float32).reshape(-1)


def row_sum(values):
    return lax.psum(values, "col")


def norm_shard(values, gain, shift):
    centre = row_sum(jnp.sum(values, axis=1)) / D
    centered = values - centre[:, None]
    spread = row_sum(jnp.sum(centered * centered, axis=1)) / D
    inverse = lax.rsqrt(spread + EPSILON)
    scaled = centered * inverse[:, None]
    return (scaled * gain + shift, scaled, inverse)


def spread_rows(values):
    return lax.all_gather(values, "col", axis=1, tiled=True)


def gather_grads(values):
    return lax.all_gather(values, "col", axis=1, tiled=True)


def norm_back(partial_rows, scaled, inverse, gain):
    shard = lax.psum_scatter(partial_rows, "col", scatter_dimension=1, tiled=True)
    grad_gain = jnp.sum(shard * scaled, axis=0)
    grad_shift = jnp.sum(shard, axis=0)
    upstream = shard * gain
    first_sum, second_sum = lax.psum(
        (jnp.sum(upstream, axis=1), jnp.sum(upstream * scaled, axis=1)), "col"
    )
    result = inverse[:, None] * (
        upstream - first_sum[:, None] / D - scaled * (second_sum[:, None] / D)
    )
    return (result, grad_gain, grad_shift)


def attend(parts):
    query, keyset, valueset = parts
    scores = times_transposed(query, keyset) * HD ** (-0.5)
    highest = jnp.max(scores, axis=1, keepdims=True)
    weights = jnp.exp(scores - highest)
    totals = jnp.sum(weights, axis=1, keepdims=True)
    chances = (weights / totals).astype(jnp.bfloat16)
    result = jnp.dot(chances, valueset, preferred_element_type=jnp.float32)
    return (result.astype(jnp.bfloat16), (highest + jnp.log(totals))[:, 0])


def attend_back(parts):
    query, keyset, valueset, upstream, logsum = parts
    scale = HD ** (-0.5)
    scores = times_transposed(query, keyset) * scale
    chances = jnp.exp(scores - logsum[:, None])
    grad_chances = times_transposed(upstream, valueset)
    grad_value = inner_rows(chances.astype(jnp.bfloat16), upstream)
    inner = jnp.sum(grad_chances * chances, axis=1, keepdims=True)
    grad_scores = (chances * (grad_chances - inner)).astype(jnp.bfloat16)
    grad_query = jnp.dot(grad_scores, keyset, preferred_element_type=jnp.float32) * scale
    grad_key = inner_rows(grad_scores, query) * scale
    return jnp.stack([grad_query, grad_key, grad_value], axis=1).astype(jnp.bfloat16)


def body(
    inputs,
    mixer_weight,
    mixer_bias,
    merge_weight,
    merge_bias,
    expand_weight,
    expand_bias,
    reduce_weight,
    reduce_bias,
    first_gain,
    first_shift,
    second_gain,
    second_shift,
    cotangent,
):
    (
        mixer_mat,
        mixer_vec,
        merge_mat,
        merge_vec,
        expand_mat,
        expand_vec,
        reduce_mat,
        reduce_vec,
        gain_one,
        shift_one,
        gain_two,
        shift_two,
    ) = (
        lax.all_gather(mixer_weight.astype(jnp.bfloat16), "row", axis=0, tiled=True),
        lax.all_gather(mixer_bias.astype(jnp.bfloat16), "row", axis=1, tiled=True),
        lax.all_gather(merge_weight.astype(jnp.bfloat16), "row", axis=0, tiled=True),
        lax.all_gather(merge_bias.astype(jnp.bfloat16), "row", axis=1, tiled=True),
        lax.all_gather(expand_weight.astype(jnp.bfloat16), "row", axis=0, tiled=True),
        lax.all_gather(expand_bias.astype(jnp.bfloat16), "row", axis=1, tiled=True),
        lax.all_gather(reduce_weight.astype(jnp.bfloat16), "row", axis=0, tiled=True),
        lax.all_gather(reduce_bias.astype(jnp.bfloat16), "row", axis=1, tiled=True),
        lax.all_gather(first_gain.astype(jnp.bfloat16), "row", axis=1, tiled=True),
        lax.all_gather(first_shift.astype(jnp.bfloat16), "row", axis=1, tiled=True),
        lax.all_gather(second_gain.astype(jnp.bfloat16), "row", axis=1, tiled=True),
        lax.all_gather(second_shift.astype(jnp.bfloat16), "row", axis=1, tiled=True),
    )
    rows = to_rows(inputs).astype(jnp.float32)
    cotan_rows = to_rows(cotangent)
    tokens = rows.shape[0]
    width = rows.shape[1]
    clips = tokens // LEN
    local_heads = width // HD
    hidden_width = expand_mat.shape[1]
    gain_first = as_vector(gain_one)
    gain_second = as_vector(gain_two)
    normed_one, scaled_one, inverse_one = norm_shard(rows, gain_first, as_vector(shift_one))
    full_one = spread_rows(normed_one.astype(jnp.bfloat16))
    pairs = mixer_vec.astype(jnp.float32).reshape(local_heads, 2, HD)
    full_bias = jnp.stack([pairs[:, 0], jnp.zeros_like(pairs[:, 0]), pairs[:, 1]], axis=1).reshape(
        -1
    )
    mixed = (jnp.dot(full_one, mixer_mat, preferred_element_type=jnp.float32) + full_bias).astype(
        jnp.bfloat16
    )
    blocks = (
        mixed.reshape(clips, LEN, local_heads, 3, HD)
        .transpose(3, 0, 2, 1, 4)
        .reshape(3, clips * local_heads, LEN, HD)
    )
    head_blocks, logsums = lax.map(attend, (blocks[0], blocks[1], blocks[2]))
    heads = (
        head_blocks.reshape(clips, local_heads, LEN, HD)
        .transpose(0, 2, 1, 3)
        .reshape(tokens, width)
    )
    branch = lax.psum_scatter(
        jnp.dot(heads, merge_mat, preferred_element_type=jnp.float32),
        "col",
        scatter_dimension=1,
        tiled=True,
    )
    state = rows + branch + as_vector(merge_vec)
    normed_two, scaled_two, inverse_two = norm_shard(state, gain_second, as_vector(shift_two))
    full_two = spread_rows(normed_two.astype(jnp.bfloat16))
    hidden = jnp.dot(full_two, expand_mat, preferred_element_type=jnp.float32) + as_vector(
        expand_vec
    )
    active = exact_gelu(hidden).astype(jnp.bfloat16)
    down = lax.psum_scatter(
        jnp.dot(active, reduce_mat, preferred_element_type=jnp.float32).astype(jnp.bfloat16),
        "col",
        scatter_dimension=1,
        tiled=True,
    ).astype(jnp.float32)
    outputs = from_rows((state + down + as_vector(reduce_vec)).astype(jnp.bfloat16))
    cotan_full = gather_grads(cotan_rows)
    grad_reduce_mat = inner_rows(active, cotan_full)
    grad_reduce_vec = jnp.sum(cotan_rows.astype(jnp.float32), axis=0)
    grad_active = times_transposed(cotan_full, reduce_mat)
    gelu_pull = jax.vjp(exact_gelu, hidden)[1]
    grad_hidden = gelu_pull(grad_active)[0].astype(jnp.bfloat16)
    grad_expand_mat = inner_rows(full_two, grad_hidden)
    grad_expand_vec = jnp.sum(grad_hidden.astype(jnp.float32), axis=0)
    back_two, grad_gain_two, grad_shift_two = norm_back(
        times_transposed(grad_hidden, expand_mat), scaled_two, inverse_two, gain_second
    )
    grad_state = cotan_rows.astype(jnp.float32) + back_two
    grad_branch = grad_state.astype(jnp.bfloat16)
    branch_full = gather_grads(grad_branch)
    grad_merge_mat = inner_rows(heads, branch_full)
    grad_merge_vec = jnp.sum(grad_branch.astype(jnp.float32), axis=0)
    grad_heads = times_transposed(branch_full, merge_mat).astype(jnp.bfloat16)
    grad_blocks = (
        grad_heads.reshape(clips, LEN, local_heads, HD)
        .transpose(0, 2, 1, 3)
        .reshape(clips * local_heads, LEN, HD)
    )
    mixed_grads = lax.map(attend_back, (blocks[0], blocks[1], blocks[2], grad_blocks, logsums))
    grad_mixed = (
        mixed_grads.reshape(clips, local_heads, LEN, 3, HD)
        .transpose(0, 2, 1, 3, 4)
        .reshape(tokens, 3 * width)
    )
    grad_mixer_mat = inner_rows(full_one, grad_mixed)
    bias_sums = jnp.sum(grad_mixed.astype(jnp.float32), axis=0).reshape(local_heads, 3, HD)
    grad_mixer_vec = jnp.stack([bias_sums[:, 0], bias_sums[:, 2]], axis=1).reshape(
        local_heads, 2 * HD
    )
    back_one, grad_gain_one, grad_shift_one = norm_back(
        times_transposed(grad_mixed, mixer_mat), scaled_one, inverse_one, gain_first
    )
    input_grad = from_rows(grad_state + back_one)
    (
        part_mixer_mat,
        part_mixer_vec,
        part_merge_mat,
        part_merge_vec,
        part_expand_mat,
        part_expand_vec,
        part_reduce_mat,
        part_reduce_vec,
        part_gain_one,
        part_shift_one,
        part_gain_two,
        part_shift_two,
    ) = (
        lax.psum_scatter(grad_mixer_mat, "row", scatter_dimension=0, tiled=True),
        lax.psum_scatter(grad_mixer_vec, "row", scatter_dimension=1, tiled=True),
        lax.psum_scatter(grad_merge_mat, "row", scatter_dimension=0, tiled=True),
        lax.psum_scatter(
            grad_merge_vec.reshape(local_heads, HD), "row", scatter_dimension=1, tiled=True
        ),
        lax.psum_scatter(grad_expand_mat, "row", scatter_dimension=0, tiled=True),
        lax.psum_scatter(
            grad_expand_vec.reshape(local_heads, hidden_width // local_heads),
            "row",
            scatter_dimension=1,
            tiled=True,
        ),
        lax.psum_scatter(grad_reduce_mat, "row", scatter_dimension=0, tiled=True),
        lax.psum_scatter(
            grad_reduce_vec.reshape(local_heads, HD), "row", scatter_dimension=1, tiled=True
        ),
        lax.psum_scatter(
            grad_gain_one.reshape(local_heads, HD), "row", scatter_dimension=1, tiled=True
        ),
        lax.psum_scatter(
            grad_shift_one.reshape(local_heads, HD), "row", scatter_dimension=1, tiled=True
        ),
        lax.psum_scatter(
            grad_gain_two.reshape(local_heads, HD), "row", scatter_dimension=1, tiled=True
        ),
        lax.psum_scatter(
            grad_shift_two.reshape(local_heads, HD), "row", scatter_dimension=1, tiled=True
        ),
    )
    summed = lax.psum(
        (
            part_mixer_mat,
            part_mixer_vec,
            part_merge_mat,
            part_merge_vec,
            part_expand_mat,
            part_expand_vec,
            part_reduce_mat,
            part_reduce_vec,
            part_gain_one,
            part_shift_one,
            part_gain_two,
            part_shift_two,
        ),
        "dp",
    )
    return (
        outputs,
        input_grad,
        summed[0],
        summed[1],
        summed[2],
        summed[3],
        summed[4],
        summed[5],
        summed[6],
        summed[7],
        summed[8],
        summed[9],
        summed[10],
        summed[11],
    )


def solution(mesh):
    in_specs = (
        P(("dp", "row"), "col", None),
        P("row", "col"),
        P("col", "row"),
        P(("col", "row"), None),
        P("col", "row"),
        P("row", "col"),
        P("col", "row"),
        P(("col", "row"), None),
        P("col", "row"),
        P("col", "row"),
        P("col", "row"),
        P("col", "row"),
        P("col", "row"),
        P(("dp", "row"), "col", None),
    )
    out_specs = (
        P(("dp", "row"), "col", None),
        P(("dp", "row"), "col", None),
        P("row", "col"),
        P("col", "row"),
        P(("col", "row"), None),
        P("col", "row"),
        P("row", "col"),
        P("col", "row"),
        P(("col", "row"), None),
        P("col", "row"),
        P("col", "row"),
        P("col", "row"),
        P("col", "row"),
        P("col", "row"),
    )
    return jax.shard_map(body, mesh=mesh, in_specs=in_specs, out_specs=out_specs, check_vma=False)
```

profile of v0, /device:TPU:0, one launch (start us, length us, event | category | flops | bytes accessed | tf_op | source)
XLA Modules:
  0.0 1910.4 jit_solution(16474213476146647296)
XLA Ops:
  9.4 6.0 all-gather.1
  15.6 5.4 all-gather
  26.0 19.2 %psum.140 = f32[3642]{0:T(1024)S(1)} all-reduce(f32[3642]{0:T(1024)S(1)} %reduce_sum.167), channel_id=1, replica_groups=mesh['dp'=2,'row'=4,'col'=4] {'col'}, use_global_device_ids=true, to_apply=%region_1.0 | all-reduce | flops 3642 | bytes 29136 | tf_op jit(solution)/shard_map/psum | solution.py:49
  47.6 15.6 psum.141
  63.2 7.0 copy.134
  70.2 9.2 reshape.237
  84.7 5.1 all-gather.2
  90.3 6.0 all_gather.53
  96.3 10.2 all_gather.51
  106.5 82.4 %all-gather.15.cloned.1.call-done = bf16[3642,768]{0,1:T(8,128)(2,1)} async-done(((bf16[3642,192]{0,1:T(8,128)(2,1)}), bf16[3642,768]{0,1:T(8,128)(2,1)}) %all-gather.15.cloned.1.call-update) | async-done | bytes 5594128 | tf_op jit(solution)/shard_map/all_gather | solution.py:62
  188.9 8.5 add_convert_fusion.1
  197.5 14.2 reshape.217
  211.7 5.4 fusion.59
  224.7 5.2 copy.171
  229.9 64.2 %while.22 = (s32[]{:T(128)}, bf16[9,1214,64]{1,2,0:T(8,128)(2,1)}, f32[9,1214]{1,0:T(8,128)}, bf16[9,1214,64]{2,1,0:T(8,128)(2,1)}, bf16[9,1214,64]{2,1,0:T(8,12...) while((s32[]{:T(128)}, bf16[9,1214,64]{1,2,0:T(8,128)(2,1)}, f32[9,1214]{1,0:T(8,128)}, ...), condition=%wide.region_7.8_spmd, body=%wide.region_4.7_spmd.sunk | while | flops 387684832 | bytes 18843696 | solution.py:174
  303.9 7.4 fusion.62
  313.3 5.1 all-gather.5
  318.5 5.1 all-gather.4
  323.8 5.1 all-gather.3
  329.1 173.6 %reduce-scatter.33.cloned.1.call-done = f32[3642,192]{0,1:T(8,128)} async-done(((f32[3642,768]{0,1:T(8,128)}), f32[3642,192]{0,1:T(8,128)}) %reduce-scatter.33.cloned.1.call-update) | async-done | bytes 2797072 | tf_op jit(solution)/shard_map/reduce_scatter | solution.py:180
  505.7 18.5 psum.142
  524.5 15.5 psum.143
  546.7 6.0 copy.158
  552.7 7.8 reshape.223
  564.4 5.1 all-gather.6
  569.6 76.5 %all-gather.17.cloned.1.call-done = bf16[3642,768]{0,1:T(8,128)(2,1)} async-done(((bf16[3642,192]{0,1:T(8,128)(2,1)}), bf16[3642,768]{0,1:T(8,128)(2,1)}) %all-gather.17.cloned.1.call-update) | async-done | bytes 5594128 | tf_op jit(solution)/shard_map/all_gather | solution.py:62
  646.1 11.6 fusion.63
  657.7 6.0 all-gather.21.cloned.1.call-done
  663.7 107.1 %all-gather.23.cloned.1.call-done = bf16[3642,768]{0,1:T(8,128)(2,1)} async-done(((bf16[3642,192]{0,1:T(8,128)(2,1)}), bf16[3642,768]{0,1:T(8,128)(2,1)}) %all-gather.23.cloned.1.call-update) | async-done | bytes 5594128 | tf_op jit(solution)/shard_map/all_gather | solution.py:66
  770.8 35.6 %convert_reduce_fusion.1 = (f32[768]{0:T(1024)S(1)}, bf16[3642,768]{1,0:T(8,128)(2,1)S(1)}, f32[3642,768]{1,0:T(8,128)}) fusion(f32[3642,768]{1,0:T(8,128)} %fusion.63, f32[768]{0:T(1024)S(1)} %reshape.245, bf16[3642,768]{0,1:T(8,128)(2,1)} %all-gather.23.cloned.1.call-done, bf16[768,768]{1,0:T(8,128)(2,1)} %all-gather.21.cloned.1.call-done), kind=kOutput, calls=%fused_computation.57 | convolution fusion | flops 4506056704 | bytes 34750464 | tf_op jit(solution)/shard_map/dot_general | solution.py:39
  808.7 7.5 fusion.64
  816.5 190.9 %reduce-scatter.37.cloned.1.call-done = f32[3642,192]{0,1:T(8,128)} async-done(((f32[3642,768]{0,1:T(8,128)}), f32[3642,192]{0,1:T(8,128)}) %reduce-scatter.37.cloned.1.call-update) | async-done | bytes 2797072 | tf_op jit(solution)/shard_map/reduce_scatter | solution.py:70
  1011.0 18.8 all-reduce.1
  1034.8 104.1 %all-gather.25.cloned.1.call-done = bf16[3642,768]{0,1:T(8,128)(2,1)} async-done(((bf16[3642,192]{0,1:T(8,128)(2,1)}), bf16[3642,768]{0,1:T(8,128)(2,1)}) %all-gather.25.cloned.1.call-update) | async-done | bytes 5594128 | tf_op jit(solution)/shard_map/all_gather | solution.py:66
  1150.2 102.2 %while.23 = (s32[]{:T(128)}, bf16[9,1214,3,64]{1,3,2,0:T(8,128)(2,1)}, bf16[9,1214,64]{2,1,0:T(8,128)(2,1)}, bf16[9,1214,64]{2,1,0:T(8,128)(2,1)}, f32[9,1214]{1...) while((s32[]{:T(128)}, ...), condition=%wide.region_21.22_spmd, body=%wide.region_19.21_spmd.sunk | while | flops 956805568 | bytes 48504736 | solution.py:222
  1252.4 8.6 copy.207
  1261.0 12.2 reshape.227
  1273.2 9.8 fusion.65
  1288.1 11.1 multiply_convert_fusion.1
  1300.1 8.2 convert_reduce_fusion
  1309.5 10.5 fusion.69
  1320.1 10.5 fusion.68
  1330.7 5.2 fusion.67
  1336.1 10.0 fusion.66
  1346.2 9.2 convolution_convert_fusion
  1355.5 118.8 %reduce-scatter.39.cloned.1.call-done = f32[3642,192]{0,1:T(8,128)} async-done(((f32[3642,768]{0,1:T(8,128)}), f32[3642,192]{0,1:T(8,128)}) %reduce-scatter.39.cloned.1.call-update) | async-done | bytes 2797072 | tf_op jit(solution)/shard_map/reduce_scatter | solution.py:70
  1479.7 5.1 all-gather.7
  1485.8 12.0 reduce-scatter.55.cloned.1.call-done
  1498.6 21.8 %reduce-scatter.53.cloned.1.call-done = f32[64,3]{1,0:T(8,128)} async-done(((f32[256,3]{1,0:T(8,128)}), f32[64,3]{1,0:T(8,128)}) %reduce-scatter.53.cloned.1.call-update) | async-done | bytes 784
  1521.1 21.1 %reduce-scatter.63.cloned.1.call-done = f32[16,3]{1,0:T(8,128)} async-done(((f32[64,3]{1,0:T(8,128)}), f32[16,3]{1,0:T(8,128)}) %reduce-scatter.63.cloned.1.call-update) | async-done | bytes 208
  1543.0 21.2 %reduce-scatter.61.cloned.1.call-done = f32[16,3]{1,0:T(8,128)} async-done(((f32[64,3]{1,0:T(8,128)}), f32[16,3]{1,0:T(8,128)}) %reduce-scatter.61.cloned.1.call-update) | async-done | bytes 208
  1565.0 21.8 %reduce-scatter.51.cloned.1.call-done = f32[16,3]{1,0:T(8,128)} async-done(((f32[64,3]{1,0:T(8,128)}), f32[16,3]{1,0:T(8,128)}) %reduce-scatter.51.cloned.1.call-update) | async-done | bytes 208
  1587.5 21.6 %reduce-scatter.49.cloned.1.call-done = f32[32,3]{1,0:T(8,128)} async-done(((f32[128,3]{1,0:T(8,128)}), f32[32,3]{1,0:T(8,128)}) %reduce-scatter.49.cloned.1.call-update) | async-done | bytes 400
  1610.0 34.6 %reduce-scatter.47.cloned.1.call-done = f32[192,768]{1,0:T(8,128)} async-done(((f32[768,768]{1,0:T(8,128)}), f32[192,768]{1,0:T(8,128)}) %reduce-scatter.47.cloned.1.call-update) | async-done | bytes 589840 | tf_op jit(solution)/shard_map/reduce_scatter | solution.py:264
  1644.6 35.8 %reduce-scatter.45.cloned.1.call-done = f32[192,768]{1,0:T(8,128)} async-done(((f32[768,768]{1,0:T(8,128)}), f32[192,768]{1,0:T(8,128)}) %reduce-scatter.45.cloned.1.call-update) | async-done | bytes 589840 | tf_op jit(solution)/shard_map/reduce_scatter | solution.py:257
  1680.4 25.2 %reduce-scatter.43.cloned.1.call-done = f32[48,768]{1,0:T(8,128)} async-done(((f32[192,768]{1,0:T(8,128)}), f32[48,768]{1,0:T(8,128)}) %reduce-scatter.43.cloned.1.call-update) | async-done | bytes 147472 | tf_op jit(solution)/shard_map/reduce_scatter | solution.py:253
  1705.6 32.8 %reduce-scatter.41.cloned.1.call-done = f32[192,576]{1,0:T(8,128)} async-done(((f32[768,576]{1,0:T(8,128)}), f32[192,576]{1,0:T(8,128)}) %reduce-scatter.41.cloned.1.call-update) | async-done | bytes 442384 | tf_op jit(solution)/shard_map/reduce_scatter | solution.py:251
  1738.4 20.2 %all-reduce = (f32[3642]{0:T(1024)S(1)}, f32[3642]{0:T(1024)S(1)}) all-reduce(f32[3642]{0:T(1024)S(1)} %get-tuple-element.185, f32[3642]{0:T(1024)S(1)} %get-tuple-element.186), channel_id=1, replica_groups=mesh['dp'=2,'row'=4,'col'=4] {'col'}, use_global_device_ids=true, to_apply=%region_26.27 | all-reduce | flops 7284 | bytes 58272 | tf_op jit(solution)/shard_map/psum | solution.py:74
  1758.7 83.7 %reduce-scatter.35.cloned.1.call-done = bf16[3642,192]{0,1:T(8,128)(2,1)} async-done(((bf16[3642,768]{0,1:T(8,128)(2,1)}), bf16[3642,192]{0,1:T(8,128)(2,1)}) %reduce-scatter.35.cloned.1.call-update) | async-done | bytes 1398544 | tf_op jit(solution)/shard_map/reduce_scatter | solution.py:193
  1842.4 6.6 multiply_add_fusion
  1849.0 5.0 copy.167
  1864.1 8.7 reshape.228
  1872.8 5.4 copy.168
  1887.1 8.7 all-reduce.2
  (359 shorter events, 281.6 us)
Async XLA Ops:
  8.0 180.9 %all-gather.15.cloned.1.call-start = ((), (), s32[]{:S(2)}) async-start(), calls=%async_computation.16 | async-start | bytes 7127040 | tf_op jit(solution)/shard_map/all_gather | solution.py:62
  21.2 61.8 %copy-start.25 = (f32[192]{0:T(256)}, f32[192]{0:T(256)S(1)}, u32[]{:S(2)}) copy-start(f32[192]{0:T(256)S(1)} %reshape.238) | copy-start | bytes 2308
  45.1 37.8 %copy-start.14 = (f32[3642]{0:T(1024)}, f32[3642]{0:T(1024)S(1)}, u32[]{:S(2)}) copy-start(f32[3642]{0:T(1024)S(1)} %broadcast_multiply_fusion.5) | copy-start | bytes 43708
  63.2 19.8 %copy-start.16 = (f32[3642]{0:T(1024)}, f32[3642]{0:T(1024)S(1)}, u32[]{:S(2)}) copy-start(f32[3642]{0:T(1024)S(1)} %add_rsqrt_fusion.1) | copy-start | bytes 43708
  83.0 23.5 %copy-start.2 = (f32[3642,192]{0,1:T(8,128)}, f32[3642,192]{0,1:T(8,128)S(1)}, u32[]{:S(2)}) copy-start(f32[3642,192]{0,1:T(8,128)S(1)} %copy.149) | copy-start | bytes 8391172
  83.0 1.7 copy-start.27
  83.0 7.2 copy-start.18
  83.0 7.2 copy-start.11
  84.6 418.0 %reduce-scatter.33.cloned.1.call-start = ((), (), s32[]{:S(2)}) async-start(), calls=%async_computation.17 | async-start | bytes 14254080 | tf_op jit(solution)/shard_map/reduce_scatter | solution.py:180
  294.1 17.2 copy-start.3
  311.3 1.1 copy-start.8
  311.3 1.9 copy-start.28
  311.3 1.9 copy-start.29
  311.3 1.9 copy-start.30
  311.4 258.2 %all-gather.19.cloned.1.call-start = ((), (), s32[]{:S(2)}) async-start(), calls=%async_computation.19 | async-start | bytes 1474560 | tf_op jit(solution)/shard_map/all_gather | solution.py:142
  313.2 332.9 %all-gather.17.cloned.1.call-start = ((), (), s32[]{:S(2)}) async-start(), calls=%async_computation.18 | async-start | bytes 7127040 | tf_op jit(solution)/shard_map/all_gather | solution.py:62
  323.8 706.2 %copy-start.23 = (f32[192]{0:T(256)}, f32[192]{0:T(256)S(1)}, u32[]{:S(2)}) copy-start(f32[192]{0:T(256)S(1)} %reshape.243) | copy-start | bytes 2308
  505.7 524.3 %copy-start = (f32[3642,192]{0,1:T(8,128)}, f32[3642,192]{0,1:T(8,128)S(1)}, u32[]{:S(2)}) copy-start(f32[3642,192]{0,1:T(8,128)S(1)} %get-tuple-element.238) | copy-start | bytes 8391172
  524.2 505.7 %copy-start.9 = (f32[3642]{0:T(1024)}, f32[3642]{0:T(1024)S(1)}, u32[]{:S(2)}) copy-start(f32[3642]{0:T(1024)S(1)} %broadcast_multiply_fusion.4) | copy-start | bytes 43708
  540.1 489.9 %copy-start.12 = (f32[3642]{0:T(1024)}, f32[3642]{0:T(1024)S(1)}, u32[]{:S(2)}) copy-start(f32[3642]{0:T(1024)S(1)} %add_rsqrt_fusion) | copy-start | bytes 43708
  541.8 121.9 %all-gather.21.cloned.1.call-start = ((), (), s32[]{:S(2)}) async-start(), calls=%async_computation.20 | async-start | bytes 1474560 | tf_op jit(solution)/shard_map/all_gather | solution.py:144
  543.7 227.1 %all-gather.23.cloned.1.call-start = ((), (), s32[]{:S(2)}) async-start(), calls=%async_computation.22 | async-start | bytes 7127040 | tf_op jit(solution)/shard_map/all_gather | solution.py:66
  560.5 3.9 copy-start.31
  564.3 443.1 %reduce-scatter.37.cloned.1.call-start = ((), (), s32[]{:S(2)}) async-start(), calls=%async_computation.23 | async-start | bytes 14254080 | tf_op jit(solution)/shard_map/reduce_scatter | solution.py:70
  770.8 38.0 %copy-start.34 = (bf16[768,768]{1,0:T(8,128)(2,1)S(1)}, bf16[768,768]{1,0:T(8,128)(2,1)}, u32[]{:S(2)}) copy-start(bf16[768,768]{1,0:T(8,128)(2,1)} %all-gather.19.cloned.1.call-done) | copy-start | bytes 3538948
  806.3 2.4 copy-start.35
  816.3 322.6 %all-gather.25.cloned.1.call-start = ((), (), s32[]{:S(2)}) async-start(), calls=%async_computation.24 | async-start | bytes 7127040 | tf_op jit(solution)/shard_map/all_gather | solution.py:66
  1029.9 4.8 copy-start.19
  1029.9 4.8 copy-start.21
  1034.7 439.6 %reduce-scatter.39.cloned.1.call-start = ((), (), s32[]{:S(2)}) async-start(), calls=%async_computation.25 | async-start | bytes 14254080 | tf_op jit(solution)/shard_map/reduce_scatter | solution.py:70
  1261.0 12.2 copy-start.7
  1283.0 1.4 copy-start.4
  1283.0 214.8 %reduce-scatter.55.cloned.1.call-start = ((), (), s32[]{:S(2)}) async-start(), calls=%async_computation.33 | async-start | bytes 40960
  1285.4 234.9 %reduce-scatter.53.cloned.1.call-start = ((), (), s32[]{:S(2)}) async-start(), calls=%async_computation.32 | async-start | bytes 163840
  1286.3 256.0 %reduce-scatter.63.cloned.1.call-start = ((), (), s32[]{:S(2)}) async-start(), calls=%async_computation.37 | async-start | bytes 40960
  1287.2 277.1 %reduce-scatter.61.cloned.1.call-start = ((), (), s32[]{:S(2)}) async-start(), calls=%async_computation.36 | async-start | bytes 40960
  1288.0 298.7 %reduce-scatter.51.cloned.1.call-start = ((), (), s32[]{:S(2)}) async-start(), calls=%async_computation.31 | async-start | bytes 40960
  1300.0 309.2 %reduce-scatter.49.cloned.1.call-start = ((), (), s32[]{:S(2)}) async-start(), calls=%async_computation.30 | async-start | bytes 81920
  1309.1 335.5 %reduce-scatter.47.cloned.1.call-start = ((), (), s32[]{:S(2)}) async-start(), calls=%async_computation.29 | async-start | bytes 2949120 | tf_op jit(solution)/shard_map/reduce_scatter | solution.py:264
  1320.0 10.6 copy-start.5
  1320.0 360.4 %reduce-scatter.45.cloned.1.call-start = ((), (), s32[]{:S(2)}) async-start(), calls=%async_computation.28 | async-start | bytes 2949120 | tf_op jit(solution)/shard_map/reduce_scatter | solution.py:257
  1330.6 375.0 %reduce-scatter.43.cloned.1.call-start = ((), (), s32[]{:S(2)}) async-start(), calls=%async_computation.27 | async-start | bytes 737280 | tf_op jit(solution)/shard_map/reduce_scatter | solution.py:253
  1335.9 10.3 copy-start.33
  1335.9 402.5 %reduce-scatter.41.cloned.1.call-start = ((), (), s32[]{:S(2)}) async-start(), calls=%async_computation.26 | async-start | bytes 2457600 | tf_op jit(solution)/shard_map/reduce_scatter | solution.py:251
  1346.2 496.2 %reduce-scatter.35.cloned.1.call-start = ((), (), s32[]{:S(2)}) async-start(), calls=%async_computation.21 | async-start | bytes 7127040 | tf_op jit(solution)/shard_map/reduce_scatter | solution.py:193
  1355.4 118.9 %copy-start.15 = (f32[3642]{0:T(1024)S(1)}, f32[3642]{0:T(1024)}, u32[]{:S(2)}) copy-start(f32[3642]{0:T(1024)} %copy-done.14) | copy-start | bytes 43708
  1355.4 118.9 %copy-start.17 = (f32[3642]{0:T(1024)S(1)}, f32[3642]{0:T(1024)}, u32[]{:S(2)}) copy-start(f32[3642]{0:T(1024)} %copy-done.16) | copy-start | bytes 43708
  1355.4 118.9 %copy-start.26 = (f32[192]{0:T(256)S(1)}, f32[192]{0:T(256)}, u32[]{:S(2)}) copy-start(f32[192]{0:T(256)} %copy-done.25) | copy-start | bytes 2308
  1355.4 124.2 %copy-start.32 = (f32[3,16]{1,0:T(4,128)S(1)}, f32[3,16]{1,0:T(4,128)}, u32[]{:S(2)}) copy-start(f32[3,16]{1,0:T(4,128)} %param.26) | copy-start | bytes 580
  1355.4 486.9 %copy-start.1 = (f32[3642,192]{0,1:T(8,128)S(1)}, f32[3642,192]{0,1:T(8,128)}, u32[]{:S(2)}) copy-start(f32[3642,192]{0,1:T(8,128)} %copy-done) | copy-start | bytes 8391172
  1355.4 486.9 %copy-start.10 = (f32[3642]{0:T(1024)S(1)}, f32[3642]{0:T(1024)}, u32[]{:S(2)}) copy-start(f32[3642]{0:T(1024)} %copy-done.9) | copy-start | bytes 43708
  1355.5 486.9 %copy-start.13 = (f32[3642]{0:T(1024)S(1)}, f32[3642]{0:T(1024)}, u32[]{:S(2)}) copy-start(f32[3642]{0:T(1024)} %copy-done.12) | copy-start | bytes 43708
  1355.5 486.9 %copy-start.20 = (f32[3642]{0:T(1024)S(1)}, f32[3642]{0:T(1024)}, u32[]{:S(2)}) copy-start(f32[3642]{0:T(1024)} %copy-done.19) | copy-start | bytes 43708
  1355.5 486.9 %copy-start.22 = (f32[3642]{0:T(1024)S(1)}, f32[3642]{0:T(1024)}, u32[]{:S(2)}) copy-start(f32[3642]{0:T(1024)} %copy-done.21) | copy-start | bytes 43708
  1355.5 486.9 %copy-start.24 = (f32[192]{0:T(256)S(1)}, f32[192]{0:T(256)}, u32[]{:S(2)}) copy-start(f32[192]{0:T(256)} %copy-done.23) | copy-start | bytes 2308
  1355.5 525.1 %reduce-scatter.59.cloned.1.call-start = ((), (), s32[]{:S(2)}) async-start(), calls=%async_computation.35 | async-start | bytes 40960
  1479.6 406.7 %reduce-scatter.57.cloned.1.call-start = ((), (), s32[]{:S(2)}) async-start(), calls=%async_computation.34 | async-start | bytes 40960
  1485.6 410.2 %all-reduce.6.cloned.1.call-start = ((), (), s32[]{:S(2)}) async-start(), calls=%async_computation.38 | async-start | bytes 3637248 | tf_op jit(solution)/shard_map/psum | solution.py:281
  1849.0 5.0 copy-start.6
Sparse Core Ops, SparseCore 0:
  84.8 104.1 all-gather.14
  311.5 191.0 reduce-scatter.32
  1034.8 104.0 all-gather.24
  1283.1 191.1 reduce-scatter.38
  1477.1 20.6 reduce-scatter.54
  1500.6 19.6 reduce-scatter.52
  1522.7 19.5 reduce-scatter.62
  1544.7 19.5 reduce-scatter.60
  1567.2 19.5 reduce-scatter.50
  1589.6 19.5 reduce-scatter.48
  1611.7 32.8 reduce-scatter.46
  1647.5 32.8 reduce-scatter.44
  1683.5 22.0 reduce-scatter.42
  1708.0 30.3 reduce-scatter.40
  1740.6 101.7 reduce-scatter.34
  1844.6 19.8 reduce-scatter.58
  1866.7 19.5 reduce-scatter.56
Sparse Core Ops, SparseCore 1:
  314.0 15.6 all-gather.18
  541.9 104.1 all-gather.16
  648.1 15.5 all-gather.20
  665.3 105.4 all-gather.22
  816.4 191.0 reduce-scatter.36
  1738.5 56.7 all-reduce.5
where the time goes:
time: 1920 us; the launch traced here: 1910 us
  waiting for transfers between devices  1200 us (62%)
  matrix products  251 us (13%)
  local copies, waits for them, and re-layouts  193 us (10%)
  blocking collectives  175 us (9%)
  other arithmetic  76.7 us (4%)
    reduce_scatter x2, waiting for transfers between devices, norm_back(): lax.psum_scatter(partial_rows, 'col', scatter_dimension=1, tiled=True)  310 us
    all_gather x2, waiting for transfers between devices, gather_grads(): return lax.all_gather(values, 'col', axis=1, tiled=True)  211 us
    reduce_scatter x1, waiting for transfers between devices, body(): lax.psum_scatter(jnp.dot(heads, merge_mat, preferred_element_type=jnp.flo...  174 us
    all_gather x2, waiting for transfers between devices, spread_rows(): return lax.all_gather(values, 'col', axis=1, tiled=True)  159 us
    unnamed x31, waiting for transfers between devices  125 us
    dot_general x31, matrix products, times_transposed(): lax.dot_general(left, right, (((1,), (1,)), ((), ())), preferred_element_...  111 us
    reduce_scatter x1, waiting for transfers between devices, body(): lax.psum_scatter(jnp.dot(active, reduce_mat, preferred_element_type=jnp.f...  83.7 us
    psum x4, blocking collectives, row_sum(): return lax.psum(values, 'col')  68.8 us
  transfers between devices with their start and end apart: 23, of which 20 were waited for; matrix products, arithmetic and copies ran while one was open for 8% of the time, Pallas kernels for 0%

commit v1 on v0

--- a/solution.py
+++ b/solution.py
@@ -7,6 +7,19 @@
 HD = 64
 LEN = 1214
 EPSILON = 1e-06
+
+
+def gather_around(array, axis, dim):
+    ways = lax.axis_size(axis)
+    up = [(d, (d + 1) % ways) for d in range(ways)]
+    down = [(d, (d - 1) % ways) for d in range(ways)]
+    earlier, later = ([array], [array])
+    for _ in range(ways // 2):
+        earlier.append(lax.ppermute(earlier[-1], axis, up))
+    for _ in range((ways - 1) // 2):
+        later.append(lax.ppermute(later[-1], axis, down))
+    line = jnp.concatenate([*earlier[::-1], *later[1:]], axis=dim)
+    return jnp.roll(line, (lax.axis_index(axis) - ways // 2) * array.shape[dim], axis=dim)
 
 
 def to_rows(values):
@@ -63,7 +76,7 @@
 
 
 def gather_grads(values):
-    return lax.all_gather(values, "col", axis=1, tiled=True)
+    return gather_around(values, "col", 1)
 
 
 def norm_back(partial_rows, scaled, inverse, gain):

time: 1920 us -> 1950 us (1.016)
  waiting for transfers between devices: 1200 us -> 1070 us
  starting transfers between devices: 1.72 us -> 84 us
  other arithmetic: 76.7 us -> 137 us
    all_gather x2 -> x0, waiting for transfers between devices: 211 us -> none  [gather_grads(): return lax.all_gather(values, 'col', axis=1, tiled=True)]
    ppermute x0 -> x6, waiting for transfers between devices: none -> 171 us  [the longest x4 167 us: gather_around(): earlier.append(lax.ppermute(earlier[-1], axis, up))]
    ppermute x0 -> x6, starting transfers between devices: none -> 82.4 us  [the longest x4 74.8 us: gather_around(): earlier.append(lax.ppermute(earlier[-1], axis, up))]
    all_gather x2, waiting for transfers between devices: 159 us -> 82.4 us  [spread_rows(): return lax.all_gather(values, 'col', axis=1, tiled=True)]
    concatenate x0 -> x2, other arithmetic: none -> 60 us  [gather_around(): jnp.roll(line, (lax.axis_index(axis) - ways // 2) * array.shape[dim], axi...]
    unnamed x31 -> x29, waiting for transfers between devices: 125 us -> 125 us
  transfers between devices with their start and end apart: 23 -> 27, of which waited for: 20 -> 21; matrix products, arithmetic and copies ran while one was open for 8% -> 10% of each run, Pallas kernels for 0% -> 0%
where the time goes in v1:
time: 1950 us; the launch traced here: 1940 us
  waiting for transfers between devices  1070 us (55%)
  matrix products  246 us (13%)
  local copies, waits for them, and re-layouts  206 us (11%)
  blocking collectives  174 us (9%)
  other arithmetic  137 us (7%)
  starting transfers between devices  84 us (4%)
    reduce_scatter x2, waiting for transfers between devices, norm_back(): lax.psum_scatter(partial_rows, 'col', scatter_dimension=1, tiled=True)  311 us
    reduce_scatter x1, waiting for transfers between devices, body(): lax.psum_scatter(jnp.dot(heads, merge_mat, preferred_element_type=jnp.flo...  174 us
    ppermute x4, waiting for transfers between devices, gather_around(): earlier.append(lax.ppermute(earlier[-1], axis, up))  167 us
    unnamed x29, waiting for transfers between devices  125 us
    dot_general x31, matrix products, times_transposed(): lax.dot_general(left, right, (((1,), (1,)), ((), ())), preferred_element_...  105 us
    reduce_scatter x1, waiting for transfers between devices, body(): lax.psum_scatter(jnp.dot(active, reduce_mat, preferred_element_type=jnp.f...  83.9 us
    all_gather x2, waiting for transfers between devices, spread_rows(): return lax.all_gather(values, 'col', axis=1, tiled=True)  82.4 us
    ppermute x4, starting transfers between devices, gather_around(): earlier.append(lax.ppermute(earlier[-1], axis, up))  74.8 us
  transfers between devices with their start and end apart: 27, of which 21 were waited for; matrix products, arithmetic and copies ran while one was open for 10% of the time, Pallas kernels for 0%

profile of v1, /device:TPU:0, one launch (start us, length us, event | category | flops | bytes accessed | tf_op | source)
XLA Modules:
  0.0 1939.3 jit_solution(14020042399139519086)
XLA Ops:
  9.4 6.0 all-gather.1
  15.6 5.4 all-gather
  26.0 19.2 psum.140
  47.6 15.6 psum.141
  63.2 7.0 copy.138
  70.2 9.2 reshape.237
  85.1 5.1 all-gather.2
  90.7 6.0 all_gather.47
  96.7 10.2 all_gather.45
  106.9 82.4 %all-gather.13.cloned.1.call-done = bf16[3642,768]{0,1:T(8,128)(2,1)} async-done(((bf16[3642,192]{0,1:T(8,128)(2,1)}), bf16[3642,768]{0,1:T(8,128)(2,1)}) %all-gather.13.cloned.1.call-update) | async-done | bytes 5594128 | tf_op jit(solution)/shard_map/all_gather | solution.py:75
  189.3 8.5 add_convert_fusion.1
  197.9 14.5 reshape.217
  212.4 5.4 fusion.73
  225.4 5.2 copy.179
  230.6 64.2 %while.22 = (s32[]{:T(128)}, bf16[9,1214,64]{1,2,0:T(8,128)(2,1)}, f32[9,1214]{1,0:T(8,128)}, bf16[9,1214,64]{2,1,0:T(8,128)(2,1)}, bf16[9,1214,64]{2,1,0:T(8,12...) while((s32[]{:T(128)}, bf16[9,1214,64]{1,2,0:T(8,128)(2,1)}, f32[9,1214]{1,0:T(8,128)}, ...), condition=%wide.region_7.8_spmd, body=%wide.region_4.7_spmd.sunk | while | flops 387684832 | bytes 18843696 | solution.py:187
  304.6 7.4 fusion.76
  324.5 5.1 all-gather.3
  329.8 173.6 %reduce-scatter.33.cloned.1.call-done = f32[3642,192]{0,1:T(8,128)} async-done(((f32[3642,768]{0,1:T(8,128)}), f32[3642,192]{0,1:T(8,128)}) %reduce-scatter.33.cloned.1.call-update) | async-done | bytes 2797072 | tf_op jit(solution)/shard_map/reduce_scatter | solution.py:193
  506.4 18.5 psum.142
  525.3 15.5 psum.143
  545.3 6.0 copy.162
  551.3 7.9 reshape.223
  566.8 62.9 %collective-permute-done = bf16[3642,192]{0,1:T(8,128)(2,1)} collective-permute-done((bf16[3642,192]{0,1:T(8,128)(2,1)}, bf16[3642,192]{0,1:T(8,128)(2,1)}, u32[]{:S(2)}, u32[]{:S(2)}) %collective-permute-start) | collective-permute-done | bytes 1398560 | tf_op jit(solution)/shard_map/ppermute | solution.py:18
  629.7 51.7 %collective-permute-start.1 = (bf16[3642,192]{0,1:T(8,128)(2,1)}, bf16[3642,192]{0,1:T(8,128)(2,1)}, u32[]{:S(2)}, u32[]{:S(2)}) collective-permute-start(bf16[3642,192]{0,1:T(8,128)(2,1)} %collective-permute-done), channel_id=1, source_target_pairs={{0,1},{1,2},{2,3},{3,0},{4,5},{5,6},{6,7},{7,4},{8,9},{9,10},{10,1... | collective-permute-start | bytes 4195592 | tf_op jit(solution)/shard_map/ppermute | solution.py:18
  695.8 42.1 %collective-permute-done.1 = bf16[3642,192]{0,1:T(8,128)(2,1)} collective-permute-done((bf16[3642,192]{0,1:T(8,128)(2,1)}, bf16[3642,192]{0,1:T(8,128)(2,1)}, u32[]{:S(2)}, u32[]{:S(2)}) %collective-permute-start.1) | collective-permute-done | bytes 1398560 | tf_op jit(solution)/shard_map/ppermute | solution.py:18
  741.5 31.6 %fusion.63 = bf16[3642,768]{1,0:T(8,128)(2,1)} fusion(s32[]{:T(128)S(6)} %select_n.13, bf16[3642,192]{1,0:T(8,128)(2,1)} %copy.166, bf16[3642,192]{1,0:T(8,128)(2,1)} %copy.167, bf16[3642,192]{1,0:T(8,128)(2,1)} %reshape.223, bf16[3642,192]{1,0:T(8,128)(2,1)} %copy.168), kind=kLoop, calls=%fused_computation.102 | loop fusion | flops 44752896 | bytes 11188228 | tf_op jit(solution)/shard_map/jit(_roll_dynamic)/concatenate | solution.py:22
  773.1 11.6 fusion.77
  784.8 32.6 %convert_reduce_fusion.1 = (f32[768]{0:T(1024)S(1)}, bf16[3642,768]{1,0:T(8,128)(2,1)S(1)}, f32[3642,768]{1,0:T(8,128)}) fusion(f32[3642,768]{1,0:T(8,128)} %fusion.77, f32[768]{0:T(1024)S(1)} %reshape.245, bf16[3642,768]{1,0:T(8,128)(2,1)} %fusion.63, bf16[768,768]{1,0:T(8,128)(2,1)} %all-gather.19.cloned.1.call-done), kind=kOutput, calls=%fused_computation.73 | convolution fusion | flops 4506056704 | bytes 34750464 | tf_op jit(solution)/shard_map/dot_general | solution.py:52
  819.8 7.5 fusion.78
  827.4 192.1 %reduce-scatter.37.cloned.1.call-done = f32[3642,192]{0,1:T(8,128)} async-done(((f32[3642,768]{0,1:T(8,128)}), f32[3642,192]{0,1:T(8,128)}) %reduce-scatter.37.cloned.1.call-update) | async-done | bytes 2797072 | tf_op jit(solution)/shard_map/reduce_scatter | solution.py:83
  1023.1 18.8 all-reduce.1
  1050.5 32.3 %collective-permute-done.3 = bf16[3642,192]{0,1:T(8,128)(2,1)S(1)} collective-permute-done((bf16[3642,192]{0,1:T(8,128)(2,1)}, bf16[3642,192]{0,1:T(8,128)(2,1)S(1)}, u32[]{:S(2)}, u32[]{:S(2)}) %collective-permute-start.3) | collective-permute-done | bytes 1398560 | tf_op jit(solution)/shard_map/ppermute | solution.py:18
  1082.8 23.1 %collective-permute-start.4 = (bf16[3642,192]{0,1:T(8,128)(2,1)S(1)}, bf16[3642,192]{0,1:T(8,128)(2,1)}, u32[]{:S(2)}, u32[]{:S(2)}) collective-permute-start(bf16[3642,192]{0,1:T(8,128)(2,1)S(1)} %collective-permute-done.3), channel_id=1, source_target_pairs={{0,1},{1,2},{2,3},{3,0},{4,5},{5,6},{6,7},{7,4},{8,9},{9,10},{10,1... | collective-permute-start | bytes 4195592 | tf_op jit(solution)/shard_map/ppermute | solution.py:18
  1109.7 29.6 %collective-permute-done.4 = bf16[3642,192]{0,1:T(8,128)(2,1)} collective-permute-done((bf16[3642,192]{0,1:T(8,128)(2,1)S(1)}, bf16[3642,192]{0,1:T(8,128)(2,1)}, u32[]{:S(2)}, u32[]{:S(2)}) %collective-permute-start.4) | collective-permute-done | bytes 1398560 | tf_op jit(solution)/shard_map/ppermute | solution.py:18
  1139.3 28.5 %fusion.56 = bf16[3642,768]{0,1:T(8,128)(2,1)S(1)} fusion(s32[]{:T(128)S(6)} %select_n.13, bf16[3642,192]{0,1:T(8,128)(2,1)} %collective-permute-done.4, bf16[3642,192]{0,1:T(8,128)(2,1)S(1)} %collective-permute-done.3, bf16[3642,192]{0,1:T(8,128)(2,1)} %get-tuple-element.237, bf16[3642,192]{0,1:T(8,128)(2,1)S(1)} %collective-permute-done.5), kind=kLoop, calls=%fused_computation.95 | loop fusion | flops 44752896 | bytes 11188228 | tf_op jit(solution)/shard_map/jit(_roll_dynamic)/concatenate | solution.py:22
  1179.0 102.5 %while.23 = (s32[]{:T(128)}, bf16[9,1214,3,64]{1,3,2,0:T(8,128)(2,1)}, bf16[9,1214,64]{2,1,0:T(8,128)(2,1)}, bf16[9,1214,64]{2,1,0:T(8,128)(2,1)}, f32[9,1214]{1...) while((s32[]{:T(128)}, ...), condition=%wide.region_21.23_spmd, body=%wide.region_19.22_spmd.sunk | while | flops 956805568 | bytes 48504736 | solution.py:235
  1281.5 8.6 copy.215
  1290.0 12.2 reshape.227
  1302.3 9.6 fusion.79
  1317.4 10.9 multiply_convert_fusion.1
  1329.2 8.2 convert_reduce_fusion
  1338.2 10.5 fusion.83
  1349.0 10.5 fusion.82
  1359.6 5.2 fusion.81
  1364.9 10.0 fusion.80
  1374.9 9.2 convolution_convert_fusion
  1384.5 118.5 %reduce-scatter.39.cloned.1.call-done = f32[3642,192]{0,1:T(8,128)} async-done(((f32[3642,768]{0,1:T(8,128)}), f32[3642,192]{0,1:T(8,128)}) %reduce-scatter.39.cloned.1.call-update) | async-done | bytes 2797072 | tf_op jit(solution)/shard_map/reduce_scatter | solution.py:83
  1514.4 11.9 reduce-scatter.55.cloned.1.call-done
  1527.2 21.8 %reduce-scatter.53.cloned.1.call-done = f32[64,3]{1,0:T(8,128)} async-done(((f32[256,3]{1,0:T(8,128)}), f32[64,3]{1,0:T(8,128)}) %reduce-scatter.53.cloned.1.call-update) | async-done | bytes 784
  1549.7 21.0 %reduce-scatter.63.cloned.1.call-done = f32[16,3]{1,0:T(8,128)} async-done(((f32[64,3]{1,0:T(8,128)}), f32[16,3]{1,0:T(8,128)}) %reduce-scatter.63.cloned.1.call-update) | async-done | bytes 208
  1571.5 21.2 %reduce-scatter.61.cloned.1.call-done = f32[16,3]{1,0:T(8,128)} async-done(((f32[64,3]{1,0:T(8,128)}), f32[16,3]{1,0:T(8,128)}) %reduce-scatter.61.cloned.1.call-update) | async-done | bytes 208
  1593.5 21.8 %reduce-scatter.51.cloned.1.call-done = f32[16,3]{1,0:T(8,128)} async-done(((f32[64,3]{1,0:T(8,128)}), f32[16,3]{1,0:T(8,128)}) %reduce-scatter.51.cloned.1.call-update) | async-done | bytes 208
  1616.0 21.8 %reduce-scatter.49.cloned.1.call-done = f32[32,3]{1,0:T(8,128)} async-done(((f32[128,3]{1,0:T(8,128)}), f32[32,3]{1,0:T(8,128)}) %reduce-scatter.49.cloned.1.call-update) | async-done | bytes 400
  1638.6 34.4 %reduce-scatter.47.cloned.1.call-done = f32[192,768]{1,0:T(8,128)} async-done(((f32[768,768]{1,0:T(8,128)}), f32[192,768]{1,0:T(8,128)}) %reduce-scatter.47.cloned.1.call-update) | async-done | bytes 589840 | tf_op jit(solution)/shard_map/reduce_scatter | solution.py:277
  1673.0 36.0 %reduce-scatter.45.cloned.1.call-done = f32[192,768]{1,0:T(8,128)} async-done(((f32[768,768]{1,0:T(8,128)}), f32[192,768]{1,0:T(8,128)}) %reduce-scatter.45.cloned.1.call-update) | async-done | bytes 589840 | tf_op jit(solution)/shard_map/reduce_scatter | solution.py:270
  1709.0 25.0 %reduce-scatter.43.cloned.1.call-done = f32[48,768]{1,0:T(8,128)} async-done(((f32[192,768]{1,0:T(8,128)}), f32[48,768]{1,0:T(8,128)}) %reduce-scatter.43.cloned.1.call-update) | async-done | bytes 147472 | tf_op jit(solution)/shard_map/reduce_scatter | solution.py:266
  1734.0 33.0 %reduce-scatter.41.cloned.1.call-done = f32[192,576]{1,0:T(8,128)} async-done(((f32[768,576]{1,0:T(8,128)}), f32[192,576]{1,0:T(8,128)}) %reduce-scatter.41.cloned.1.call-update) | async-done | bytes 442384 | tf_op jit(solution)/shard_map/reduce_scatter | solution.py:264
  1767.0 20.0 %all-reduce = (f32[3642]{0:T(1024)S(1)}, f32[3642]{0:T(1024)S(1)}) all-reduce(f32[3642]{0:T(1024)S(1)} %get-tuple-element.186, f32[3642]{0:T(1024)S(1)} %get-tuple-element.187), channel_id=1, replica_groups=mesh['dp'=2,'row'=4,'col'=4] {'col'}, use_global_device_ids=true, to_apply=%region_26.28 | all-reduce | flops 7284 | bytes 58272 | tf_op jit(solution)/shard_map/psum | solution.py:87
  1787.0 83.9 %reduce-scatter.35.cloned.1.call-done = bf16[3642,192]{0,1:T(8,128)(2,1)} async-done(((bf16[3642,768]{0,1:T(8,128)(2,1)}), bf16[3642,192]{0,1:T(8,128)(2,1)}) %reduce-scatter.35.cloned.1.call-update) | async-done | bytes 1398544 | tf_op jit(solution)/shard_map/reduce_scatter | solution.py:206
  1871.0 6.6 multiply_add_fusion
  1892.7 8.7 reshape.228
  1901.4 5.4 copy.176
  1909.9 5.1 reduce-scatter.57.cloned.1.call-done
  1915.8 8.7 all-reduce.2
  (372 shorter events, 324.3 us)
Async XLA Ops:
  8.0 181.3 %all-gather.13.cloned.1.call-start = ((), (), s32[]{:S(2)}) async-start(), calls=%async_computation.16 | async-start | bytes 7127040 | tf_op jit(solution)/shard_map/all_gather | solution.py:75
  21.2 61.8 %copy-start.26 = (f32[192]{0:T(256)}, f32[192]{0:T(256)S(1)}, u32[]{:S(2)}) copy-start(f32[192]{0:T(256)S(1)} %reshape.238) | copy-start | bytes 2308
  45.1 37.9 %copy-start.15 = (f32[3642]{0:T(1024)}, f32[3642]{0:T(1024)S(1)}, u32[]{:S(2)}) copy-start(f32[3642]{0:T(1024)S(1)} %broadcast_multiply_fusion.5) | copy-start | bytes 43708
  63.2 19.9 %copy-start.17 = (f32[3642]{0:T(1024)}, f32[3642]{0:T(1024)S(1)}, u32[]{:S(2)}) copy-start(f32[3642]{0:T(1024)S(1)} %add_rsqrt_fusion.1) | copy-start | bytes 43708
  79.4 5.7 copy-start.28
  79.4 11.2 copy-start.19
  79.4 11.2 copy-start.12
  83.0 114.8 %copy-start.2 = (f32[3642,192]{0,1:T(8,128)}, f32[3642,192]{0,1:T(8,128)S(1)}, u32[]{:S(2)}) copy-start(f32[3642,192]{0,1:T(8,128)S(1)} %copy.153) | copy-start | bytes 8391172
  85.1 418.3 %reduce-scatter.33.cloned.1.call-start = ((), (), s32[]{:S(2)}) async-start(), calls=%async_computation.17 | async-start | bytes 14254080 | tf_op jit(solution)/shard_map/reduce_scatter | solution.py:193
  294.8 17.2 copy-start.3
  312.0 1.1 copy-start.9
  312.0 1.9 copy-start.29
  312.0 1.9 copy-start.30
  312.0 1.9 copy-start.31
  312.1 461.0 %all-gather.17.cloned.1.call-start = ((), (), s32[]{:S(2)}) async-start(), calls=%async_computation.19 | async-start | bytes 1474560 | tf_op jit(solution)/shard_map/all_gather | solution.py:155
  313.9 459.3 %all-gather.15.cloned.1.call-start = ((), (), s32[]{:S(2)}) async-start(), calls=%async_computation.18 | async-start | bytes 7127040 | tf_op jit(solution)/shard_map/all_gather | solution.py:75
  324.5 717.5 %copy-start.24 = (f32[192]{0:T(256)}, f32[192]{0:T(256)S(1)}, u32[]{:S(2)}) copy-start(f32[192]{0:T(256)S(1)} %reshape.243) | copy-start | bytes 2308
  506.4 535.6 %copy-start = (f32[3642,192]{0,1:T(8,128)}, f32[3642,192]{0,1:T(8,128)S(1)}, u32[]{:S(2)}) copy-start(f32[3642,192]{0,1:T(8,128)S(1)} %get-tuple-element.239) | copy-start | bytes 8391172
  524.9 517.0 %copy-start.10 = (f32[3642]{0:T(1024)}, f32[3642]{0:T(1024)S(1)}, u32[]{:S(2)}) copy-start(f32[3642]{0:T(1024)S(1)} %broadcast_multiply_fusion.4) | copy-start | bytes 43708
  540.8 501.2 %copy-start.13 = (f32[3642]{0:T(1024)}, f32[3642]{0:T(1024)S(1)}, u32[]{:S(2)}) copy-start(f32[3642]{0:T(1024)S(1)} %add_rsqrt_fusion) | copy-start | bytes 43708
  542.5 242.3 %all-gather.19.cloned.1.call-start = ((), (), s32[]{:S(2)}) async-start(), calls=%async_computation.20 | async-start | bytes 1474560 | tf_op jit(solution)/shard_map/all_gather | solution.py:157
  551.3 131.9 %copy-start.32 = (f32[3,64]{1,0:T(4,128)S(1)}, f32[3,64]{1,0:T(4,128)}, u32[]{:S(2)}) copy-start(f32[3,64]{1,0:T(4,128)} %param.26) | copy-start | bytes 2308
  562.9 66.8 %collective-permute-start = (bf16[3642,192]{0,1:T(8,128)(2,1)}, bf16[3642,192]{0,1:T(8,128)(2,1)}, u32[]{:S(2)}, u32[]{:S(2)}) collective-permute-start(bf16[3642,192]{0,1:T(8,128)(2,1)} %copy.163), channel_id=1, source_target_pairs={{0,1},{1,2},{2,3},{3,0},{4,5},{5,6},{6,7},{7,4},{8,9},{9,10},{10,1... | collective-permute-start | bytes 4195592 | tf_op jit(solution)/shard_map/ppermute | solution.py:18
  563.0 129.1 %collective-permute-start.2 = (bf16[3642,192]{0,1:T(8,128)(2,1)}, bf16[3642,192]{0,1:T(8,128)(2,1)}, u32[]{:S(2)}, u32[]{:S(2)}) collective-permute-start(bf16[3642,192]{0,1:T(8,128)(2,1)} %copy.163), channel_id=1, source_target_pairs={{0,3},{1,0},{2,1},{3,2},{4,7},{5,4},{6,5},{7,6},{8,11},{9,8},{10,9... | collective-permute-start | bytes 4195592 | tf_op jit(solution)/shard_map/ppermute | solution.py:20
  629.7 108.2 %collective-permute-start.1 = (bf16[3642,192]{0,1:T(8,128)(2,1)}, bf16[3642,192]{0,1:T(8,128)(2,1)}, u32[]{:S(2)}, u32[]{:S(2)}) collective-permute-start(bf16[3642,192]{0,1:T(8,128)(2,1)} %collective-permute-done), channel_id=1, source_target_pairs={{0,1},{1,2},{2,3},{3,0},{4,5},{5,6},{6,7},{7,4},{8,9},{9,10},{10,1... | collective-permute-start | bytes 4195592 | tf_op jit(solution)/shard_map/ppermute | solution.py:18
  683.2 336.3 %reduce-scatter.37.cloned.1.call-start = ((), (), s32[]{:S(2)}) async-start(), calls=%async_computation.22 | async-start | bytes 14254080 | tf_op jit(solution)/shard_map/reduce_scatter | solution.py:83
  784.8 35.0 %copy-start.35 = (bf16[768,768]{1,0:T(8,128)(2,1)S(1)}, bf16[768,768]{1,0:T(8,128)(2,1)}, u32[]{:S(2)}) copy-start(bf16[768,768]{1,0:T(8,128)(2,1)} %all-gather.17.cloned.1.call-done) | copy-start | bytes 3538948
  817.4 2.4 copy-start.36
  827.4 675.6 %reduce-scatter.39.cloned.1.call-start = ((), (), s32[]{:S(2)}) async-start(), calls=%async_computation.23 | async-start | bytes 14254080 | tf_op jit(solution)/shard_map/reduce_scatter | solution.py:83
  1041.9 40.9 %copy-start.20 = (f32[3642]{0:T(1024)}, f32[3642]{0:T(1024)S(1)}, u32[]{:S(2)}) copy-start(f32[3642]{0:T(1024)S(1)} %get-tuple-element.253) | copy-start | bytes 43708
  1041.9 40.9 %copy-start.22 = (f32[3642]{0:T(1024)}, f32[3642]{0:T(1024)S(1)}, u32[]{:S(2)}) copy-start(f32[3642]{0:T(1024)S(1)} %get-tuple-element.254) | copy-start | bytes 43708
  1046.7 36.1 %collective-permute-start.3 = (bf16[3642,192]{0,1:T(8,128)(2,1)}, bf16[3642,192]{0,1:T(8,128)(2,1)S(1)}, u32[]{:S(2)}, u32[]{:S(2)}) collective-permute-start(bf16[3642,192]{0,1:T(8,128)(2,1)} %get-tuple-element.237), channel_id=1, source_target_pairs={{0,1},{1,2},{2,3},{3,0},{4,5},{5,6},{6,7},{7,4},{8,9},{9,10},{10,1... | collective-permute-start | bytes 4195592 | tf_op jit(solution)/shard_map/ppermute | solution.py:18
  1046.7 63.0 %collective-permute-start.5 = (bf16[3642,192]{0,1:T(8,128)(2,1)}, bf16[3642,192]{0,1:T(8,128)(2,1)S(1)}, u32[]{:S(2)}, u32[]{:S(2)}) collective-permute-start(bf16[3642,192]{0,1:T(8,128)(2,1)} %get-tuple-element.237), channel_id=1, source_target_pairs={{0,3},{1,0},{2,1},{3,2},{4,7},{5,4},{6,5},{7,6},{8,11},{9,8},{10,9... | collective-permute-start | bytes 4195592 | tf_op jit(solution)/shard_map/ppermute | solution.py:20
  1082.8 56.5 %collective-permute-start.4 = (bf16[3642,192]{0,1:T(8,128)(2,1)S(1)}, bf16[3642,192]{0,1:T(8,128)(2,1)}, u32[]{:S(2)}, u32[]{:S(2)}) collective-permute-start(bf16[3642,192]{0,1:T(8,128)(2,1)S(1)} %collective-permute-done.3), channel_id=1, source_target_pairs={{0,1},{1,2},{2,3},{3,0},{4,5},{5,6},{6,7},{7,4},{8,9},{9,10},{10,1... | collective-permute-start | bytes 4195592 | tf_op jit(solution)/shard_map/ppermute | solution.py:18
  1167.8 2.4 copy-start.6
  1290.0 12.2 copy-start.8
  1311.9 1.4 copy-start.4
  1311.9 214.5 %reduce-scatter.55.cloned.1.call-start = ((), (), s32[]{:S(2)}) async-start(), calls=%async_computation.31 | async-start | bytes 40960
  1314.3 234.6 %reduce-scatter.53.cloned.1.call-start = ((), (), s32[]{:S(2)}) async-start(), calls=%async_computation.30 | async-start | bytes 163840
  1315.2 255.6 %reduce-scatter.63.cloned.1.call-start = ((), (), s32[]{:S(2)}) async-start(), calls=%async_computation.35 | async-start | bytes 40960
  1316.4 276.2 %reduce-scatter.61.cloned.1.call-start = ((), (), s32[]{:S(2)}) async-start(), calls=%async_computation.34 | async-start | bytes 40960
  1317.3 297.9 %reduce-scatter.51.cloned.1.call-start = ((), (), s32[]{:S(2)}) async-start(), calls=%async_computation.29 | async-start | bytes 40960
  1329.1 308.7 %reduce-scatter.49.cloned.1.call-start = ((), (), s32[]{:S(2)}) async-start(), calls=%async_computation.28 | async-start | bytes 81920
  1338.1 334.9 %reduce-scatter.47.cloned.1.call-start = ((), (), s32[]{:S(2)}) async-start(), calls=%async_computation.27 | async-start | bytes 2949120 | tf_op jit(solution)/shard_map/reduce_scatter | solution.py:277
  1348.7 10.8 copy-start.5
  1348.8 360.3 %reduce-scatter.45.cloned.1.call-start = ((), (), s32[]{:S(2)}) async-start(), calls=%async_computation.26 | async-start | bytes 2949120 | tf_op jit(solution)/shard_map/reduce_scatter | solution.py:270
  1359.5 374.5 %reduce-scatter.43.cloned.1.call-start = ((), (), s32[]{:S(2)}) async-start(), calls=%async_computation.25 | async-start | bytes 737280 | tf_op jit(solution)/shard_map/reduce_scatter | solution.py:266
  1364.8 10.1 copy-start.34
  1364.8 402.2 %reduce-scatter.41.cloned.1.call-start = ((), (), s32[]{:S(2)}) async-start(), calls=%async_computation.24 | async-start | bytes 2457600 | tf_op jit(solution)/shard_map/reduce_scatter | solution.py:264
  1374.9 496.1 %reduce-scatter.35.cloned.1.call-start = ((), (), s32[]{:S(2)}) async-start(), calls=%async_computation.21 | async-start | bytes 7127040 | tf_op jit(solution)/shard_map/reduce_scatter | solution.py:206
  1384.1 118.9 %copy-start.16 = (f32[3642]{0:T(1024)S(1)}, f32[3642]{0:T(1024)}, u32[]{:S(2)}) copy-start(f32[3642]{0:T(1024)} %copy-done.15) | copy-start | bytes 43708
  1384.1 118.9 %copy-start.18 = (f32[3642]{0:T(1024)S(1)}, f32[3642]{0:T(1024)}, u32[]{:S(2)}) copy-start(f32[3642]{0:T(1024)} %copy-done.17) | copy-start | bytes 43708
  1384.1 118.9 %copy-start.27 = (f32[192]{0:T(256)S(1)}, f32[192]{0:T(256)}, u32[]{:S(2)}) copy-start(f32[192]{0:T(256)} %copy-done.26) | copy-start | bytes 2308
  1384.1 124.2 %copy-start.33 = (f32[3,16]{1,0:T(4,128)S(1)}, f32[3,16]{1,0:T(4,128)}, u32[]{:S(2)}) copy-start(f32[3,16]{1,0:T(4,128)} %param.28) | copy-start | bytes 580
  1384.1 486.8 %copy-start.1 = (f32[3642,192]{0,1:T(8,128)S(1)}, f32[3642,192]{0,1:T(8,128)}, u32[]{:S(2)}) copy-start(f32[3642,192]{0,1:T(8,128)} %copy-done) | copy-start | bytes 8391172
  1384.1 486.8 %copy-start.11 = (f32[3642]{0:T(1024)S(1)}, f32[3642]{0:T(1024)}, u32[]{:S(2)}) copy-start(f32[3642]{0:T(1024)} %copy-done.10) | copy-start | bytes 43708
  1384.1 486.8 %copy-start.14 = (f32[3642]{0:T(1024)S(1)}, f32[3642]{0:T(1024)}, u32[]{:S(2)}) copy-start(f32[3642]{0:T(1024)} %copy-done.13) | copy-start | bytes 43708
  1384.1 486.8 %copy-start.21 = (f32[3642]{0:T(1024)S(1)}, f32[3642]{0:T(1024)}, u32[]{:S(2)}) copy-start(f32[3642]{0:T(1024)} %copy-done.20) | copy-start | bytes 43708
  1384.1 486.8 %copy-start.23 = (f32[3642]{0:T(1024)S(1)}, f32[3642]{0:T(1024)}, u32[]{:S(2)}) copy-start(f32[3642]{0:T(1024)} %copy-done.22) | copy-start | bytes 43708
  1384.2 486.8 %copy-start.25 = (f32[192]{0:T(256)S(1)}, f32[192]{0:T(256)}, u32[]{:S(2)}) copy-start(f32[192]{0:T(256)} %copy-done.24) | copy-start | bytes 2308
  1384.2 524.9 %reduce-scatter.59.cloned.1.call-start = ((), (), s32[]{:S(2)}) async-start(), calls=%async_computation.33 | async-start | bytes 40960
  1508.3 406.7 %reduce-scatter.57.cloned.1.call-start = ((), (), s32[]{:S(2)}) async-start(), calls=%async_computation.32 | async-start | bytes 40960
  1514.2 410.3 %all-reduce.6.cloned.1.call-start = ((), (), s32[]{:S(2)}) async-start(), calls=%async_computation.36 | async-start | bytes 3637248 | tf_op jit(solution)/shard_map/psum | solution.py:294
  1877.6 5.0 copy-start.7
Sparse Core Ops, SparseCore 0:
  85.2 104.1 all-gather.12
  312.2 191.0 reduce-scatter.32
  1312.0 190.8 reduce-scatter.38
  1505.8 20.5 reduce-scatter.54
  1529.2 19.6 reduce-scatter.52
  1551.2 19.5 reduce-scatter.62
  1573.1 19.5 reduce-scatter.60
  1595.7 19.5 reduce-scatter.50
  1618.2 19.5 reduce-scatter.48
  1640.2 32.8 reduce-scatter.46
  1676.2 32.8 reduce-scatter.44
  1711.9 22.0 reduce-scatter.42
  1736.6 30.3 reduce-scatter.40
  1769.2 101.7 reduce-scatter.34
  1873.2 19.8 reduce-scatter.58
  1895.4 19.5 reduce-scatter.56
Sparse Core Ops, SparseCore 1:
  314.7 15.6 all-gather.16
  542.6 186.5 all-gather.14
  731.2 15.7 all-gather.18
  827.4 192.0 reduce-scatter.36
  1767.1 56.7 all-reduce.5
